TPU v7x, 32 devices: a whole 2x2x4 slice. The times are simulated.
32 devices in a mesh: shard: 8 (over z, x), ctx: 2 (over core), tp: 2 (over y).
Axes of the slice: x: 2, y: 2, z: 4, core: 2. Of those that a mesh axis runs over, the one named last changes fastest.
Arguments:
- tokens: bfloat16 [2, 8, 1024, 1280], P(None, 'shard', 'ctx'), may hold values from -6 to 6
- patch_meta: int32 [3, 2, 8, 1024], P(None, None, 'shard'), may hold values from -1 to 31, as said below
- attn_norm_gain: float32 [1280], replicated, may hold values from 0.5 to 1.5
- attn_norm_bias: float32 [1280], replicated, may hold values from -3 to 3
- qkv_weight: bfloat16 [3, 1280, 1280], P(None, 'shard', 'tp'), may hold values from -0.15625 to 0.15625
- qkv_bias: float32 [3, 1280], P(None, 'tp'), may hold values from -3 to 3
- proj_weight: bfloat16 [1280, 1280], P('tp', 'shard'), may hold values from -0.625 to 0.625
- proj_bias: float32 [1280], replicated, may hold values from -3 to 3
- mlp_norm_gain: float32 [1280], replicated, may hold values from 0.5 to 1.5
- mlp_norm_bias: float32 [1280], replicated, may hold values from -3 to 3
- fc1_weight: bfloat16 [1280, 5120], P('shard', 'tp'), may hold values from -0.15625 to 0.15625
- fc1_bias: float32 [5120], P('tp'), may hold values from -3 to 3
- fc2_weight: bfloat16 [5120, 1280], P('tp', 'shard'), may hold values from -0.078125 to 0.078125
- fc2_bias: float32 [1280], replicated, may hold values from -3 to 3
- cotangent: bfloat16 [2, 8, 1024, 1280], P(None, 'shard', 'ctx'), may hold values from -6 to 6
Outputs:
- block_output: bfloat16 [2, 8, 1024, 1280], P(None, 'shard', 'ctx')
- input_grad: float32 [2, 8, 1024, 1280], P(None, 'shard', 'ctx')
- grad_attn_norm_gain: float32 [1280], replicated
- grad_attn_norm_bias: float32 [1280], replicated
- grad_qkv_weight: float32 [3, 1280, 1280], P(None, 'shard', 'tp')
- grad_qkv_bias: float32 [3, 1280], P(None, 'tp')
- grad_proj_weight: float32 [1280, 1280], P('tp', 'shard')
- grad_proj_bias: float32 [1280], replicated
- grad_mlp_norm_gain: float32 [1280], replicated
- grad_mlp_norm_bias: float32 [1280], replicated
- grad_fc1_weight: float32 [1280, 5120], P('shard', 'tp')
- grad_fc1_bias: float32 [5120], P('tp')
- grad_fc2_weight: float32 [5120, 1280], P('tp', 'shard')
- grad_fc2_bias: float32 [1280], replicated
Inputs may be any that keep to these rules, and one draw needn't show every extreme that they name: patch_meta[0] holds each slot's picture id, counting up from 0 along a packed row, and -1 on padding slots, which lie only at a row's end; patch_meta[1] and patch_meta[2] hold the patch's row and column inside its picture (0 on padding). Pictures are rectangles of 10 to 32 patches a side filled row by row; only a row's last picture may have fewer picture rows. Fewer than 32 slots of a row are padding.
All inputs are finite; a program needn't handle non-finite values.
Results may differ from a plain program's by a relative error of at most 0.012.
Values may be sent and summed in bfloat16 or wider, within the bound.
A program may use at most 256 MiB of HBM per device.

v0:
```python
import math
import jax
import jax.numpy as jnp
from jax import lax
from jax.sharding import PartitionSpec as P

HDIM = 80
norm_epsilon = 1e-06
gelu_factor = 1.702
rope_base = 10000.0


def norm_stats(values):
    center = values - jnp.mean(values, -1, keepdims=True)
    spread = jnp.mean(center * center, -1, keepdims=True)
    inverse = lax.rsqrt(spread + norm_epsilon)
    return (center * inverse, inverse)


def norm_back(grad_out, normal, inverse, gain):
    scaled = grad_out * gain
    return inverse * (
        scaled
        - jnp.mean(scaled, -1, keepdims=True)
        - normal * jnp.mean(scaled * normal, -1, keepdims=True)
    )


def rope_tables(patch_row, patch_col, head_size):
    quarter = head_size // 4
    frequency = rope_base ** (-2.0 * jnp.arange(quarter, dtype=jnp.float32) / (head_size // 2))
    angles = jnp.concatenate(
        [
            patch_row.astype(jnp.float32)[:, None] * frequency[None, :],
            patch_col.astype(jnp.float32)[:, None] * frequency[None, :],
        ],
        axis=1,
    )
    angles = jnp.concatenate([angles, angles], axis=1)
    return (jnp.cos(angles)[:, None, :], jnp.sin(angles)[:, None, :])


def rotate_half(tensor):
    half_size = tensor.shape[-1] // 2
    return jnp.concatenate([-tensor[..., half_size:], tensor[..., :half_size]], axis=-1)


def apply_rope(tensor, cosine, sine_table):
    return tensor * cosine + rotate_half(tensor) * sine_table


def undo_rope(gradient, cosine, sine_table):
    return gradient * cosine - rotate_half(gradient * sine_table)


def split_heads(flat, batch, length, head_count):
    return (
        flat.reshape(batch, length, head_count, HDIM)
        .transpose(0, 2, 1, 3)
        .reshape(batch * head_count, length, HDIM)
    )


def join_heads(items, batch, length, head_count):
    return (
        items.reshape(batch, head_count, length, HDIM)
        .transpose(0, 2, 1, 3)
        .reshape(batch, length, head_count * HDIM)
    )


def masked_logits(query_head, key_head, query_ids, key_ids):
    logits = jnp.einsum("qd,kd->qk", query_head, key_head, preferred_element_type=jnp.float32) * (
        1.0 / math.sqrt(HDIM)
    )
    return jnp.where(query_ids[:, None] == key_ids[None, :], logits, -1e30)


def attend(packed):
    query_head, key_head, value_head, query_ids, key_ids = packed
    logits = masked_logits(query_head, key_head, query_ids, key_ids)
    peak = jnp.max(logits, -1, keepdims=True)
    exponent = jnp.exp(logits - peak)
    normalizer = jnp.sum(exponent, -1, keepdims=True)
    probs_low = (exponent / normalizer).astype(jnp.bfloat16)
    mixed_head = jnp.einsum("qk,kd->qd", probs_low, value_head, preferred_element_type=jnp.float32)
    return (mixed_head.astype(jnp.bfloat16), peak[:, 0] + jnp.log(normalizer[:, 0]))


def attend_back(packed):
    query_head, key_head, value_head, query_ids, key_ids, grad_head, log_total = packed
    score_scale = 1.0 / math.sqrt(HDIM)
    logits = masked_logits(query_head, key_head, query_ids, key_ids)
    probs = jnp.exp(logits - log_total[:, None])
    d_probs = jnp.einsum("qd,kd->qk", grad_head, value_head, preferred_element_type=jnp.float32)
    inner_sum = jnp.sum(probs * d_probs, -1, keepdims=True)
    d_logits = (probs * (d_probs - inner_sum)).astype(jnp.bfloat16)
    d_query = (
        jnp.einsum("qk,kd->qd", d_logits, key_head, preferred_element_type=jnp.float32)
        * score_scale
    )
    d_key = (
        jnp.einsum("qk,qd->kd", d_logits, query_head, preferred_element_type=jnp.float32)
        * score_scale
    )
    d_value = jnp.einsum(
        "qk,qd->kd", probs.astype(jnp.bfloat16), grad_head, preferred_element_type=jnp.float32
    )
    return (d_query, d_key, d_value)


def per_device(
    tokens,
    patch_meta,
    attn_norm_gain,
    attn_norm_bias,
    qkv_weight,
    qkv_bias,
    proj_weight,
    proj_bias,
    mlp_norm_gain,
    mlp_norm_bias,
    fc1_weight,
    fc1_bias,
    fc2_weight,
    fc2_bias,
    cotangent,
):
    local_len = tokens.shape[2]
    model_width = tokens.shape[3]
    full_len = patch_meta.shape[3]
    inner_width = qkv_weight.shape[2]
    ff_local = fc1_weight.shape[1]
    head_count = inner_width // HDIM
    offset = lax.axis_index("ctx") * local_len
    full_qkv, full_proj, full_first, full_second = (
        lax.all_gather(qkv_weight, "shard", axis=1, tiled=True),
        lax.all_gather(proj_weight, "shard", axis=1, tiled=True),
        lax.all_gather(fc1_weight, "shard", axis=0, tiled=True),
        lax.all_gather(fc2_weight, "shard", axis=1, tiled=True),
    )

    def one_micro(running, sample):
        tok_one, cot_one, meta_one = sample
        ids_all = meta_one[0]
        ids_own = lax.dynamic_slice_in_dim(ids_all, offset, local_len, 1)
        own_row = lax.dynamic_slice_in_dim(meta_one[1], offset, local_len, 1).reshape(local_len)
        own_col = lax.dynamic_slice_in_dim(meta_one[2], offset, local_len, 1).reshape(local_len)
        cosine, sine_table = rope_tables(own_row, own_col, HDIM)
        inputs = tok_one.reshape(local_len, model_width).astype(jnp.float32)
        normal_one, inverse_one = norm_stats(inputs)
        normed = (normal_one * attn_norm_gain + attn_norm_bias).astype(jnp.bfloat16)
        projected = (
            jnp.einsum("rd,cde->cre", normed, full_qkv, preferred_element_type=jnp.float32)
            + qkv_bias[:, None, :]
        )
        query = apply_rope(
            projected[0].reshape(local_len, head_count, HDIM), cosine, sine_table
        ).astype(jnp.bfloat16)
        key_part = apply_rope(
            projected[1].reshape(local_len, head_count, HDIM), cosine, sine_table
        ).astype(jnp.bfloat16)
        value_part = projected[2].astype(jnp.bfloat16)
        key_all, value_all = (
            lax.all_gather(key_part.reshape(1, local_len, inner_width), "ctx", axis=1, tiled=True),
            lax.all_gather(
                value_part.reshape(1, local_len, inner_width), "ctx", axis=1, tiled=True
            ),
        )
        query_items = split_heads(query, 1, local_len, head_count)
        key_items = split_heads(key_all, 1, full_len, head_count)
        value_items = split_heads(value_all, 1, full_len, head_count)
        query_ids = jnp.repeat(ids_own, head_count, axis=0)
        key_ids = jnp.repeat(ids_all, head_count, axis=0)
        mixed_items, log_totals = lax.map(
            attend, (query_items, key_items, value_items, query_ids, key_ids)
        )
        mixed = join_heads(mixed_items, 1, local_len, head_count).reshape(local_len, inner_width)
        attn_out = (
            lax.psum(jnp.dot(mixed, full_proj, preferred_element_type=jnp.float32), "tp")
            + proj_bias
        )
        hidden = inputs + attn_out
        normal_two, inverse_two = norm_stats(hidden)
        normed_two = (normal_two * mlp_norm_gain + mlp_norm_bias).astype(jnp.bfloat16)
        pre_act = jnp.dot(normed_two, full_first, preferred_element_type=jnp.float32) + fc1_bias
        sigmoid_part = jax.nn.sigmoid(gelu_factor * pre_act)
        activated = (pre_act * sigmoid_part).astype(jnp.bfloat16)
        mlp_out = (
            lax.psum(
                jnp.dot(activated, full_second, preferred_element_type=jnp.float32).astype(
                    jnp.bfloat16
                ),
                "tp",
            ).astype(jnp.float32)
            + fc2_bias
        )
        output_one = (hidden + mlp_out).astype(jnp.bfloat16).reshape(tok_one.shape)
        back_qkv, back_proj, back_first, back_second = (
            lax.all_gather(qkv_weight, "shard", axis=1, tiled=True),
            lax.all_gather(proj_weight, "shard", axis=1, tiled=True),
            lax.all_gather(fc1_weight, "shard", axis=0, tiled=True),
            lax.all_gather(fc2_weight, "shard", axis=1, tiled=True),
        )
        grad_low = cot_one.reshape(local_len, model_width)
        grad_out = grad_low.astype(jnp.float32)
        grad_second = jnp.einsum(
            "rf,rd->fd", activated, grad_low, preferred_element_type=jnp.float32
        )
        grad_second_bias = jnp.sum(grad_out, 0)
        d_act = jnp.einsum("rd,fd->rf", grad_low, back_second, preferred_element_type=jnp.float32)
        d_pre = (
            d_act * (sigmoid_part + gelu_factor * pre_act * sigmoid_part * (1.0 - sigmoid_part))
        ).astype(jnp.bfloat16)
        grad_first = jnp.einsum("rd,rf->df", normed_two, d_pre, preferred_element_type=jnp.float32)
        grad_first_bias = jnp.sum(d_pre.astype(jnp.float32), 0)
        d_norm_two = lax.psum(
            jnp.einsum("rf,df->rd", d_pre, back_first, preferred_element_type=jnp.float32), "tp"
        )
        grad_mlp_gain = jnp.sum(d_norm_two * normal_two, 0)
        grad_mlp_shift = jnp.sum(d_norm_two, 0)
        d_hidden = grad_out + norm_back(d_norm_two, normal_two, inverse_two, mlp_norm_gain)
        d_attn = d_hidden.astype(jnp.bfloat16)
        grad_proj_bias = jnp.sum(d_attn.astype(jnp.float32), 0)
        grad_proj = jnp.einsum("re,rd->ed", mixed, d_attn, preferred_element_type=jnp.float32)
        d_mixed = jnp.einsum(
            "rd,ed->re", d_attn, back_proj, preferred_element_type=jnp.float32
        ).astype(jnp.bfloat16)
        grad_items = split_heads(d_mixed, 1, local_len, head_count)
        d_query_items, d_key_items, d_value_items = lax.map(
            attend_back,
            (query_items, key_items, value_items, query_ids, key_ids, grad_items, log_totals),
        )
        d_key_all = join_heads(d_key_items, 1, full_len, head_count)
        d_value_all = join_heads(d_value_items, 1, full_len, head_count)
        d_key_own, d_value_own = (
            lax.psum_scatter(d_key_all, "ctx", scatter_dimension=1, tiled=True),
            lax.psum_scatter(d_value_all, "ctx", scatter_dimension=1, tiled=True),
        )
        d_query = join_heads(d_query_items, 1, local_len, head_count).reshape(
            local_len, head_count, HDIM
        )
        d_query_raw = undo_rope(d_query, cosine, sine_table).reshape(local_len, inner_width)
        d_key_raw = undo_rope(
            d_key_own.reshape(local_len, head_count, HDIM), cosine, sine_table
        ).reshape(local_len, inner_width)
        d_projected = jnp.stack(
            [d_query_raw, d_key_raw, d_value_own.reshape(local_len, inner_width)]
        ).astype(jnp.bfloat16)
        grad_qkv = jnp.einsum(
            "rd,cre->cde", normed, d_projected, preferred_element_type=jnp.float32
        )
        grad_qkv_shift = jnp.sum(d_projected.astype(jnp.float32), 1)
        d_normed = lax.psum(
            jnp.einsum("cre,cde->rd", d_projected, back_qkv, preferred_element_type=jnp.float32),
            "tp",
        )
        grad_attn_gain = jnp.sum(d_normed * normal_one, 0)
        grad_attn_shift = jnp.sum(d_normed, 0)
        input_one = (
            d_hidden + norm_back(d_normed, normal_one, inverse_one, attn_norm_gain)
        ).reshape(tok_one.shape)
        fresh = (
            grad_qkv,
            grad_proj,
            grad_first,
            grad_second,
            grad_attn_gain,
            grad_attn_shift,
            grad_qkv_shift,
            grad_proj_bias,
            grad_mlp_gain,
            grad_mlp_shift,
            grad_first_bias,
            grad_second_bias,
        )
        running = jax.tree.map(lambda earlier, latest: earlier + latest, running, fresh)
        return (running, (output_one, input_one))

    start_sums = (
        jnp.zeros((3, model_width, inner_width), jnp.float32),
        jnp.zeros((inner_width, model_width), jnp.float32),
        jnp.zeros((model_width, ff_local), jnp.float32),
        jnp.zeros((ff_local, model_width), jnp.float32),
        jnp.zeros((model_width,), jnp.float32),
        jnp.zeros((model_width,), jnp.float32),
        jnp.zeros((3, inner_width), jnp.float32),
        jnp.zeros((model_width,), jnp.float32),
        jnp.zeros((model_width,), jnp.float32),
        jnp.zeros((model_width,), jnp.float32),
        jnp.zeros((ff_local,), jnp.float32),
        jnp.zeros((model_width,), jnp.float32),
    )
    totals, (block_output, input_grad) = lax.scan(
        one_micro, start_sums, (tokens, cotangent, jnp.moveaxis(patch_meta, 1, 0))
    )
    small_sums = lax.psum(
        (totals[4], totals[5], totals[6], totals[7], totals[8], totals[9], totals[10], totals[11]),
        ("shard", "ctx"),
    )
    weight_grads = (totals[0], totals[1], totals[2], totals[3])
    weight_grads = (
        lax.psum_scatter(weight_grads[0], "shard", scatter_dimension=1, tiled=True),
        lax.psum_scatter(weight_grads[1], "shard", scatter_dimension=1, tiled=True),
        lax.psum_scatter(weight_grads[2], "shard", scatter_dimension=0, tiled=True),
        lax.psum_scatter(weight_grads[3], "shard", scatter_dimension=1, tiled=True),
    )
    weight_grads = lax.psum(
        (weight_grads[0], weight_grads[1], weight_grads[2], weight_grads[3]), "ctx"
    )
    return (
        block_output,
        input_grad,
        small_sums[0],
        small_sums[1],
        weight_grads[0],
        small_sums[2],
        weight_grads[1],
        small_sums[3],
        small_sums[4],
        small_sums[5],
        weight_grads[2],
        small_sums[6],
        weight_grads[3],
        small_sums[7],
    )


def solution(mesh):
    placed = (
        P(None, "shard", "ctx", None),
        P(None, None, "shard", None),
        P(),
        P(),
        P(None, "shard", "tp"),
        P(None, "tp"),
        P("tp", "shard"),
        P(),
        P(),
        P(),
        P("shard", "tp"),
        P("tp"),
        P("tp", "shard"),
        P(),
        P(None, "shard", "ctx", None),
    )
    return jax.shard_map(
        per_device,
        mesh=mesh,
        in_specs=placed,
        out_specs=(
            P(None, "shard", "ctx", None),
            P(None, "shard", "ctx", None),
            P(),
            P(),
            P(None, "shard", "tp"),
            P(None, "tp"),
            P("tp", "shard"),
            P(),
            P(),
            P(),
            P("shard", "tp"),
            P("tp"),
            P("tp", "shard"),
            P(),
        ),
        check_vma=False,
    )
```

profile of v0, /device:TPU:0, one launch (start us, length us, event | category | flops | bytes accessed | tf_op | source)
XLA Modules:
  0.0 2368.6 jit_solution(1720924637512056237)
XLA Ops:
  11.7 46.6 %all-gather.13.cloned.1.call-done = bf16[640,1280]{0,1:T(8,128)(2,1)} async-done(((bf16[640,160]{0,1:T(8,128)(2,1)}), bf16[640,1280]{0,1:T(8,128)(2,1)}) %all-gather.13.cloned.1.call-update) | async-done | bytes 1638416 | tf_op jit(solution)/shard_map/all_gather | solution.py:138
  58.3 3.5 copy.93
  61.9 99.7 %all-gather.17.cloned.1.call-done = bf16[2560,1280]{0,1:T(8,128)(2,1)} async-done(((bf16[2560,160]{0,1:T(8,128)(2,1)}), bf16[2560,1280]{0,1:T(8,128)(2,1)}) %all-gather.17.cloned.1.call-update) | async-done | bytes 6553616 | tf_op jit(solution)/shard_map/all_gather | solution.py:140
  161.6 9.5 copy.94
  171.2 73.1 %all-gather.11.cloned.1.call-done = bf16[3,1280,640]{2,1,0:T(8,128)(2,1)} async-done(((bf16[3,160,640]{2,1,0:T(8,128)(2,1)}), bf16[3,1280,640]{2,1,0:T(8,128)(2,1)}) %all-gather.11.cloned.1.call-update) | async-done | bytes 4915216 | tf_op jit(solution)/shard_map/all_gather | solution.py:137
  244.3 102.5 %all-gather.15.cloned.1.call-done = bf16[1280,2560]{1,0:T(8,128)(2,1)} async-done(((bf16[160,2560]{1,0:T(8,128)(2,1)}), bf16[1280,2560]{1,0:T(8,128)(2,1)}) %all-gather.15.cloned.1.call-update) | async-done | bytes 6553616 | tf_op jit(solution)/shard_map/all_gather | solution.py:139
  346.9 1259.4 %while.96 = (s32[]{:T(128)}, f32[3,1280,640]{1,2,0:T(8,128)}, f32[640,1280]{1,0:T(8,128)}, f32[1280,2560]{1,0:T(8,128)}, f32[2560,1280]{1,0:T(8,128)}, /*index=5...) while((s32[]{:T(128)}, f32[3,1280,640]{1,2,0:T(8,128)}, ...), condition=%wide.region_30.31_spmd.clone, body=%wide.region_0.30_spmd.clone.sunk | while | flops 30925250560 | bytes 610404544 | solution.py:294
  347.9 5.4 add_bitcast_fusion.2
  360.9 3.6 add_convert_fusion.10
  371.7 4.5 all-gather.19.cloned.1.call-done
  380.2 40.1 %while.97 = (s32[]{:T(128)}, bf16[8,512,80]{1,2,0:T(8,128)(2,1)S(1)}, f32[8,512]{1,0:T(8,128)}, s32[8,512]{1,0:T(8,128)S(1)}, s32[8,1024]{1,0:T(8,128)S(1)}, /*i...) while((s32[]{:T(128)}, ...), condition=%wide.region_6.6_spmd, body=%wide.region_3.5_spmd.sunk | while | flops 172531200 | bytes 7069817 | solution.py:175
  420.3 4.4 fusion.163
  426.4 74.0 %all-reduce.10.cloned.1.call-done = f32[512,1280]{1,0:T(8,128)} async-done(((f32[512,1280]{1,0:T(8,128)}), f32[512,1280]{1,0:T(8,128)}) %all-reduce.10.cloned.1.call-update) | async-done | bytes 2621456 | tf_op jit(solution)/shard_map/while/body/eval_jaxpr/psum | solution.py:180
  503.4 8.4 fusion.165
  511.8 18.7 all-gather.25.cloned.1.call-done
  530.5 11.5 convert_reduce_fusion.10
  542.1 90.7 %all-gather.27.cloned.1.call-done = bf16[1280,2560]{1,0:T(8,128)(2,1)} async-done(((bf16[160,2560]{1,0:T(8,128)(2,1)}), bf16[1280,2560]{1,0:T(8,128)(2,1)}) %all-gather.27.cloned.1.call-update) | async-done | bytes 6553616 | tf_op jit(solution)/shard_map/while/body/eval_jaxpr/all_gather | solution.py:202
  632.7 8.8 fusion.166
  642.1 10.6 convolution_convert_fusion.6
  652.8 10.3 reduce-scatter.15.cloned.1.call-start
  663.1 51.0 %all-reduce.12.cloned.1.call-done = f32[512,1280]{1,0:T(8,128)} async-done(((f32[512,1280]{1,0:T(8,128)}), f32[512,1280]{1,0:T(8,128)}) %all-reduce.12.cloned.1.call-update) | async-done | bytes 2621456 | tf_op jit(solution)/shard_map/while/body/eval_jaxpr/psum | solution.py:217
  714.2 2.9 multiply_reduce_fusion.10
  719.9 4.4 convolution_convert_fusion.5
  725.7 75.7 %while.98 = (s32[]{:T(128)}, f32[8,512,80]{1,2,0:T(8,128)}, f32[8,1024,80]{1,2,0:T(8,128)}, f32[8,1024,80]{1,2,0:T(8,128)}, s32[8,512]{1,0:T(8,128)S(1)}, /*inde...) while((s32[]{:T(128)}, f32[8,512,80]{1,2,0:T(8,128)}, ...), condition=%wide.region_15.15_spmd, body=%wide.region_13.14_spmd.sunk | while | flops 424795648 | bytes 17794184 | solution.py:230
  803.0 12.0 convolution_add_fusion.8
  820.0 5.5 reduce-scatter.17.cloned.1.call-done
  831.1 55.9 %all-gather.29.cloned.1.call-done = bf16[3,1280,640]{2,1,0:T(8,128)(2,1)} async-done(((bf16[3,160,640]{2,1,0:T(8,128)(2,1)}), bf16[3,1280,640]{2,1,0:T(8,128)(2,1)}) %all-gather.29.cloned.1.call-update) | async-done | bytes 4915216 | tf_op jit(solution)/shard_map/while/body/eval_jaxpr/all_gather | solution.py:200
  887.0 7.2 convolution_bitcast_fusion.3
  894.4 9.1 convolution_add_fusion.7
  907.4 6.4 bitcast_add_fusion.2
  913.9 53.1 %all-reduce.14.cloned.1.call-done = f32[512,1280]{1,0:T(8,128)} async-done(((f32[512,1280]{1,0:T(8,128)}), f32[512,1280]{1,0:T(8,128)}) %all-reduce.14.cloned.1.call-update) | async-done | bytes 2621456 | tf_op jit(solution)/shard_map/while/body/eval_jaxpr/psum | solution.py:254
  966.9 3.0 fusion.168
  970.1 4.1 fusion.170
  975.5 5.4 add_bitcast_fusion.2
  988.5 3.4 add_convert_fusion.10
  999.0 6.5 all-gather.19.cloned.1.call-done
  1009.6 40.1 %while.97 = (s32[]{:T(128)}, bf16[8,512,80]{1,2,0:T(8,128)(2,1)S(1)}, f32[8,512]{1,0:T(8,128)}, s32[8,512]{1,0:T(8,128)S(1)}, s32[8,1024]{1,0:T(8,128)S(1)}, /*i...) while((s32[]{:T(128)}, ...), condition=%wide.region_6.6_spmd, body=%wide.region_3.5_spmd.sunk | while | flops 172531200 | bytes 7069817 | solution.py:175
  1049.7 4.4 fusion.163
  1055.8 74.0 %all-reduce.10.cloned.1.call-done = f32[512,1280]{1,0:T(8,128)} async-done(((f32[512,1280]{1,0:T(8,128)}), f32[512,1280]{1,0:T(8,128)}) %all-reduce.10.cloned.1.call-update) | async-done | bytes 2621456 | tf_op jit(solution)/shard_map/while/body/eval_jaxpr/psum | solution.py:180
  1132.8 8.4 fusion.165
  1141.2 19.1 all-gather.25.cloned.1.call-done
  1160.2 11.5 convert_reduce_fusion.10
  1171.8 90.8 %all-gather.27.cloned.1.call-done = bf16[1280,2560]{1,0:T(8,128)(2,1)} async-done(((bf16[160,2560]{1,0:T(8,128)(2,1)}), bf16[1280,2560]{1,0:T(8,128)(2,1)}) %all-gather.27.cloned.1.call-update) | async-done | bytes 6553616 | tf_op jit(solution)/shard_map/while/body/eval_jaxpr/all_gather | solution.py:202
  1262.6 8.8 fusion.166
  1272.0 10.6 convolution_convert_fusion.6
  1282.9 61.1 %all-reduce.12.cloned.1.call-done = f32[512,1280]{1,0:T(8,128)} async-done(((f32[512,1280]{1,0:T(8,128)}), f32[512,1280]{1,0:T(8,128)}) %all-reduce.12.cloned.1.call-update) | async-done | bytes 2621456 | tf_op jit(solution)/shard_map/while/body/eval_jaxpr/psum | solution.py:217
  1349.8 4.6 convolution_convert_fusion.5
  1355.7 75.8 %while.98 = (s32[]{:T(128)}, f32[8,512,80]{1,2,0:T(8,128)}, f32[8,1024,80]{1,2,0:T(8,128)}, f32[8,1024,80]{1,2,0:T(8,128)}, s32[8,512]{1,0:T(8,128)S(1)}, /*inde...) while((s32[]{:T(128)}, f32[8,512,80]{1,2,0:T(8,128)}, ...), condition=%wide.region_15.15_spmd, body=%wide.region_13.14_spmd.sunk | while | flops 424795648 | bytes 17794184 | solution.py:230
  1432.9 16.3 convolution_add_fusion.8
  1461.0 55.6 %all-gather.29.cloned.1.call-done = bf16[3,1280,640]{2,1,0:T(8,128)(2,1)} async-done(((bf16[3,160,640]{2,1,0:T(8,128)(2,1)}), bf16[3,1280,640]{2,1,0:T(8,128)(2,1)}) %all-gather.29.cloned.1.call-update) | async-done | bytes 4915216 | tf_op jit(solution)/shard_map/while/body/eval_jaxpr/all_gather | solution.py:200
  1516.6 7.2 convolution_bitcast_fusion.3
  1524.0 11.9 convolution_add_fusion.7
  1539.9 8.1 bitcast_add_fusion.2
  1548.0 48.6 %all-reduce.14.cloned.1.call-done = f32[512,1280]{1,0:T(8,128)} async-done(((f32[512,1280]{1,0:T(8,128)}), f32[512,1280]{1,0:T(8,128)}) %all-reduce.14.cloned.1.call-update) | async-done | bytes 2621456 | tf_op jit(solution)/shard_map/while/body/eval_jaxpr/psum | solution.py:254
  1596.6 3.0 fusion.168
  1599.7 4.1 fusion.170
  1606.3 4.6 copy.96
  1611.0 11.3 copy.95
  1623.1 14.0 copy.97
  1637.2 50.0 %reduce-scatter.9.cloned.1.call-done = f32[640,160]{0,1:T(8,128)} async-done(((f32[640,1280]{0,1:T(8,128)}), f32[640,160]{0,1:T(8,128)}) %reduce-scatter.9.cloned.1.call-update) | async-done | bytes 409616 | tf_op jit(solution)/shard_map/reduce_scatter | solution.py:304
  1687.2 171.9 %reduce-scatter.7.cloned.1.call-done = f32[3,160,640]{2,1,0:T(8,128)} async-done(((f32[3,1280,640]{2,1,0:T(8,128)}), f32[3,160,640]{2,1,0:T(8,128)}) %reduce-scatter.7.cloned.1.call-update) | async-done | bytes 1228816 | tf_op jit(solution)/shard_map/reduce_scatter | solution.py:303
  1859.1 217.8 %reduce-scatter.11.cloned.1.call-done = f32[160,2560]{1,0:T(8,128)} async-done(((f32[1280,2560]{1,0:T(8,128)}), f32[160,2560]{1,0:T(8,128)}) %reduce-scatter.11.cloned.1.call-update) | async-done | bytes 1638416 | tf_op jit(solution)/shard_map/reduce_scatter | solution.py:305
  2076.9 217.6 %reduce-scatter.13.cloned.1.call-done = f32[2560,160]{0,1:T(8,128)} async-done(((f32[2560,1280]{0,1:T(8,128)}), f32[2560,160]{0,1:T(8,128)}) %reduce-scatter.13.cloned.1.call-update) | async-done | bytes 1638416 | tf_op jit(solution)/shard_map/reduce_scatter | solution.py:306
  2294.7 61.0 %all-reduce = (f32[1280]{0:T(1024)}, f32[1280]{0:T(1024)}, f32[3,640]{1,0:T(4,128)}, f32[1280]{0:T(1024)}, f32[1280]{0:T(1024)}, /*index=5*/f32[1280]{0:T(1024)}, f32[2560]{0:T(1024)}, f32[1280]{0:T(1024)}) all-reduce(f32[1280]{0:T(1024)S(1)} %copy-done.55, ...), channel_id=1, replica_groups=mesh['shard'=8,'ctx'=2,'tp'=2] {'shard','ctx'}, use_global_device_ids=true, to_apply=%region_31.32 | all-reduce | flops 12160 | bytes 97280 | tf_op jit(solution)/shard_map/psum | solution.py:297
  (691 shorter events, 334.9 us)
Async XLA Ops:
  8.0 50.3 %all-gather.13.cloned.1.call-start = ((), (), s32[]{:S(2)}) async-start(), calls=%async_computation.7 | async-start | bytes 1843200 | tf_op jit(solution)/shard_map/all_gather | solution.py:138
  8.7 152.9 %all-gather.17.cloned.1.call-start = ((), (), s32[]{:S(2)}) async-start(), calls=%async_computation.9 | async-start | bytes 7372800 | tf_op jit(solution)/shard_map/all_gather | solution.py:140
  9.5 234.8 %all-gather.11.cloned.1.call-start = ((), (), s32[]{:S(2)}) async-start(), calls=%async_computation.6 | async-start | bytes 5529600 | tf_op jit(solution)/shard_map/all_gather | solution.py:137
  10.2 336.6 %all-gather.15.cloned.1.call-start = ((), (), s32[]{:S(2)}) async-start(), calls=%async_computation.8 | async-start | bytes 7372800 | tf_op jit(solution)/shard_map/all_gather | solution.py:139
  61.8 285.0 %copy-start = (bf16[2,1,512,1280]{3,2,1,0:T(8,128)(2,1)S(1)}, bf16[2,1,512,1280]{3,2,1,0:T(8,128)(2,1)}, u32[]{:S(2)}) copy-start(bf16[2,1,512,1280]{3,2,1,0:T(8,128)(2,1)} %param.21) | copy-start | bytes 7864324
  61.8 285.0 %copy-start.20 = (f32[1280]{0:T(1024)S(1)}, f32[1280]{0:T(1024)}, u32[]{:S(2)}) copy-start(f32[1280]{0:T(1024)} %param.29) | copy-start | bytes 15364
  61.8 285.0 %copy-start.21 = (f32[1280]{0:T(1024)S(1)}, f32[1280]{0:T(1024)}, u32[]{:S(2)}) copy-start(f32[1280]{0:T(1024)} %param.23) | copy-start | bytes 15364
  61.8 285.0 %copy-start.27 = (f32[1280]{0:T(1024)S(1)}, f32[1280]{0:T(1024)}, u32[]{:S(2)}) copy-start(f32[1280]{0:T(1024)} %param.30) | copy-start | bytes 15364
  61.9 285.0 %copy-start.58 = (f32[1280]{0:T(1024)S(1)}, f32[1280]{0:T(1024)}, u32[]{:S(2)}) copy-start(f32[1280]{0:T(1024)} %param.24) | copy-start | bytes 15364
  61.9 285.0 %copy-start.60 = (f32[1280]{0:T(1024)S(1)}, f32[1280]{0:T(1024)}, u32[]{:S(2)}) copy-start(f32[1280]{0:T(1024)} %param.28) | copy-start | bytes 15364
  61.9 285.0 %copy-start.62 = (f32[2560]{0:T(1024)S(1)}, f32[2560]{0:T(1024)}, u32[]{:S(2)}) copy-start(f32[2560]{0:T(1024)} %param.32) | copy-start | bytes 30724
  61.9 285.0 %copy-start.64 = (f32[3,640]{1,0:T(4,128)S(1)}, f32[3,640]{1,0:T(4,128)}, u32[]{:S(2)}) copy-start(f32[3,640]{1,0:T(4,128)} %param.26) | copy-start | bytes 23044
  347.1 20.5 copy-start.56
  347.1 20.5 all-gather.21.cloned.1.call-start
  356.3 19.8 all-gather.19.cloned.1.call-start
  364.5 135.9 %all-reduce.10.cloned.1.call-start = ((), (), s32[]{:S(2)}) async-start(), calls=%async_computation.18 | async-start | bytes 5242880 | tf_op jit(solution)/shard_map/while/body/eval_jaxpr/psum | solution.py:180
  424.7 105.8 %all-gather.25.cloned.1.call-start = ((), (), s32[]{:S(2)}) async-start(), calls=%async_computation.19 | async-start | bytes 7372800 | tf_op jit(solution)/shard_map/while/body/eval_jaxpr/all_gather | solution.py:203
  425.3 207.4 %all-gather.27.cloned.1.call-start = ((), (), s32[]{:S(2)}) async-start(), calls=%async_computation.20 | async-start | bytes 7372800 | tf_op jit(solution)/shard_map/while/body/eval_jaxpr/all_gather | solution.py:202
  425.9 288.3 %all-reduce.12.cloned.1.call-start = ((), (), s32[]{:S(2)}) async-start(), calls=%async_computation.21 | async-start | bytes 5242880 | tf_op jit(solution)/shard_map/while/body/eval_jaxpr/psum | solution.py:217
  641.5 78.4 %all-gather.23.cloned.1.call-start = ((), (), s32[]{:S(2)}) async-start(), calls=%async_computation.17 | async-start | bytes 1843200 | tf_op jit(solution)/shard_map/while/body/eval_jaxpr/all_gather | solution.py:201
  642.1 173.0 %all-reduce.16.cloned.1.call-start = ((), (), s32[]{:S(2)}) async-start(), calls=%async_computation.26 | async-start | bytes 2621440 | tf_op jit(solution)/shard_map/while/body/eval_jaxpr/psum | solution.py:190
  652.8 165.0 %reduce-scatter.15.cloned.1.call-start = ((), (), s32[]{:S(2)}) async-start(), calls=%async_computation.22 | async-start | bytes 3932160 | tf_op jit(solution)/shard_map/while/body/eval_jaxpr/reduce_scatter | solution.py:238
  801.5 24.0 %reduce-scatter.17.cloned.1.call-start = ((), (), s32[]{:S(2)}) async-start(), calls=%async_computation.23 | async-start | bytes 3932160 | tf_op jit(solution)/shard_map/while/body/eval_jaxpr/reduce_scatter | solution.py:237
  802.2 84.8 %all-gather.29.cloned.1.call-start = ((), (), s32[]{:S(2)}) async-start(), calls=%async_computation.24 | async-start | bytes 5529600 | tf_op jit(solution)/shard_map/while/body/eval_jaxpr/all_gather | solution.py:200
  802.9 164.0 %all-reduce.14.cloned.1.call-start = ((), (), s32[]{:S(2)}) async-start(), calls=%async_computation.25 | async-start | bytes 5242880 | tf_op jit(solution)/shard_map/while/body/eval_jaxpr/psum | solution.py:254
  803.0 12.0 copy-start.61
  913.8 56.1 %copy-start.50 = (f32[1280]{0:T(1024)S(1)}, f32[1280]{0:T(1024)}, u32[]{:S(2)}) copy-start(f32[1280]{0:T(1024)} %get-tuple-element.1512) | copy-start | bytes 15364 | tf_op jit(solution)/shard_map/while
  913.8 56.1 %copy-start.53 = (f32[1280]{0:T(1024)S(1)}, f32[1280]{0:T(1024)}, u32[]{:S(2)}) copy-start(f32[1280]{0:T(1024)} %get-tuple-element.1511) | copy-start | bytes 15364 | tf_op jit(solution)/shard_map/while
  913.8 56.2 %copy-start.22 = (f32[1280]{0:T(1024)S(1)}, f32[1280]{0:T(1024)}, u32[]{:S(2)}) copy-start(f32[1280]{0:T(1024)} %get-tuple-element.1772) | copy-start | bytes 15364 | tf_op jit(solution)/shard_map/while
  974.6 20.3 copy-start.56
  974.7 20.3 all-gather.21.cloned.1.call-start
  983.9 21.7 all-gather.19.cloned.1.call-start
  991.9 137.9 %all-reduce.10.cloned.1.call-start = ((), (), s32[]{:S(2)}) async-start(), calls=%async_computation.18 | async-start | bytes 5242880 | tf_op jit(solution)/shard_map/while/body/eval_jaxpr/psum | solution.py:180
  1054.1 106.1 %all-gather.25.cloned.1.call-start = ((), (), s32[]{:S(2)}) async-start(), calls=%async_computation.19 | async-start | bytes 7372800 | tf_op jit(solution)/shard_map/while/body/eval_jaxpr/all_gather | solution.py:203
  1054.9 207.7 %all-gather.27.cloned.1.call-start = ((), (), s32[]{:S(2)}) async-start(), calls=%async_computation.20 | async-start | bytes 7372800 | tf_op jit(solution)/shard_map/while/body/eval_jaxpr/all_gather | solution.py:202
  1055.6 288.4 %all-reduce.12.cloned.1.call-start = ((), (), s32[]{:S(2)}) async-start(), calls=%async_computation.21 | async-start | bytes 5242880 | tf_op jit(solution)/shard_map/while/body/eval_jaxpr/psum | solution.py:217
  1271.3 78.5 %all-gather.23.cloned.1.call-start = ((), (), s32[]{:S(2)}) async-start(), calls=%async_computation.17 | async-start | bytes 1843200 | tf_op jit(solution)/shard_map/while/body/eval_jaxpr/all_gather | solution.py:201
  1271.9 177.3 %all-reduce.16.cloned.1.call-start = ((), (), s32[]{:S(2)}) async-start(), calls=%async_computation.26 | async-start | bytes 2621440 | tf_op jit(solution)/shard_map/while/body/eval_jaxpr/psum | solution.py:190
  1282.7 169.3 %reduce-scatter.15.cloned.1.call-start = ((), (), s32[]{:S(2)}) async-start(), calls=%async_computation.22 | async-start | bytes 3932160 | tf_op jit(solution)/shard_map/while/body/eval_jaxpr/reduce_scatter | solution.py:238
  1431.5 23.9 %reduce-scatter.17.cloned.1.call-start = ((), (), s32[]{:S(2)}) async-start(), calls=%async_computation.23 | async-start | bytes 3932160 | tf_op jit(solution)/shard_map/while/body/eval_jaxpr/reduce_scatter | solution.py:237
  1432.2 84.4 %all-gather.29.cloned.1.call-start = ((), (), s32[]{:S(2)}) async-start(), calls=%async_computation.24 | async-start | bytes 5529600 | tf_op jit(solution)/shard_map/while/body/eval_jaxpr/all_gather | solution.py:200
  1432.8 163.7 %all-reduce.14.cloned.1.call-start = ((), (), s32[]{:S(2)}) async-start(), calls=%async_computation.25 | async-start | bytes 5242880 | tf_op jit(solution)/shard_map/while/body/eval_jaxpr/psum | solution.py:254
  1432.9 16.3 copy-start.61
  1523.9 12.0 copy-start.38
  1523.9 12.0 copy-start.41
  1523.9 12.1 copy-start.2
  1524.0 12.1 copy-start.11
  1524.0 12.1 copy-start.18
  1548.0 51.6 %copy-start.50 = (f32[1280]{0:T(1024)S(1)}, f32[1280]{0:T(1024)}, u32[]{:S(2)}) copy-start(f32[1280]{0:T(1024)} %get-tuple-element.1512) | copy-start | bytes 15364 | tf_op jit(solution)/shard_map/while
  1548.0 51.6 %copy-start.53 = (f32[1280]{0:T(1024)S(1)}, f32[1280]{0:T(1024)}, u32[]{:S(2)}) copy-start(f32[1280]{0:T(1024)} %get-tuple-element.1511) | copy-start | bytes 15364 | tf_op jit(solution)/shard_map/while
  1548.0 51.7 %copy-start.22 = (f32[1280]{0:T(1024)S(1)}, f32[1280]{0:T(1024)}, u32[]{:S(2)}) copy-start(f32[1280]{0:T(1024)} %get-tuple-element.1772) | copy-start | bytes 15364 | tf_op jit(solution)/shard_map/while
  1606.3 81.0 %reduce-scatter.9.cloned.1.call-start = ((), (), s32[]{:S(2)}) async-start(), calls=%async_computation.11 | async-start | bytes 3686400 | tf_op jit(solution)/shard_map/reduce_scatter | solution.py:304
  1611.0 248.1 %reduce-scatter.7.cloned.1.call-start = ((), (), s32[]{:S(2)}) async-start(), calls=%async_computation.10 | async-start | bytes 11059200 | tf_op jit(solution)/shard_map/reduce_scatter | solution.py:303
  1622.3 454.6 %reduce-scatter.11.cloned.1.call-start = ((), (), s32[]{:S(2)}) async-start(), calls=%async_computation.12 | async-start | bytes 14745600 | tf_op jit(solution)/shard_map/reduce_scatter | solution.py:305
  1623.0 671.5 %reduce-scatter.13.cloned.1.call-start = ((), (), s32[]{:S(2)}) async-start(), calls=%async_computation.13 | async-start | bytes 14745600 | tf_op jit(solution)/shard_map/reduce_scatter | solution.py:306
  1637.1 657.5 %copy-start.32 = (f32[2560]{0:T(1024)S(1)}, f32[2560]{0:T(1024)}, u32[]{:S(2)}) copy-start(f32[2560]{0:T(1024)} %get-tuple-element.1896) | copy-start | bytes 30724
  1637.1 657.5 %copy-start.36 = (f32[3,640]{1,0:T(4,128)S(1)}, f32[3,640]{1,0:T(4,128)}, u32[]{:S(2)}) copy-start(f32[3,640]{1,0:T(4,128)} %get-tuple-element.1892) | copy-start | bytes 23044
  1637.1 657.5 %copy-start.40 = (f32[1280]{0:T(1024)S(1)}, f32[1280]{0:T(1024)}, u32[]{:S(2)}) copy-start(f32[1280]{0:T(1024)} %get-tuple-element.1897) | copy-start | bytes 15364
  1637.1 657.5 %copy-start.43 = (f32[1280]{0:T(1024)S(1)}, f32[1280]{0:T(1024)}, u32[]{:S(2)}) copy-start(f32[1280]{0:T(1024)} %get-tuple-element.1895) | copy-start | bytes 15364
  1637.1 657.5 %copy-start.46 = (f32[1280]{0:T(1024)S(1)}, f32[1280]{0:T(1024)}, u32[]{:S(2)}) copy-start(f32[1280]{0:T(1024)} %get-tuple-element.1894) | copy-start | bytes 15364
  1637.2 657.5 %copy-start.49 = (f32[1280]{0:T(1024)S(1)}, f32[1280]{0:T(1024)}, u32[]{:S(2)}) copy-start(f32[1280]{0:T(1024)} %get-tuple-element.1893) | copy-start | bytes 15364
  1637.2 657.5 %copy-start.52 = (f32[1280]{0:T(1024)S(1)}, f32[1280]{0:T(1024)}, u32[]{:S(2)}) copy-start(f32[1280]{0:T(1024)} %get-tuple-element.1891) | copy-start | bytes 15364
  1637.2 657.5 %copy-start.55 = (f32[1280]{0:T(1024)S(1)}, f32[1280]{0:T(1024)}, u32[]{:S(2)}) copy-start(f32[1280]{0:T(1024)} %get-tuple-element.1890) | copy-start | bytes 15364
  1637.2 718.5 %all-reduce.8.cloned.1.call-start = ((), (), s32[]{:S(2)}) async-start(), calls=%async_computation.14 | async-start | bytes 9830400 | tf_op jit(solution)/shard_map/psum | solution.py:308
  (84 other events, 377.8 us)
Sparse Core Ops, SparseCore 0:
  11.0 47.2 all-gather.12
  60.5 101.1 all-gather.16
  163.8 80.4 all-gather.10
  246.3 100.4 all-gather.14
  356.4 7.5 all-gather.20
  365.5 10.5 all-gather.18
  424.8 75.5 all-reduce.9
  641.6 72.5 all-reduce.11
  716.6 45.7 all-reduce.15
  801.6 10.0 reduce-scatter.14
  814.0 11.4 reduce-scatter.16
  894.4 72.5 all-reduce.13
  984.0 9.4 all-gather.20
  994.9 10.5 all-gather.18
  1054.2 75.5 all-reduce.9
  1271.5 72.5 all-reduce.11
  1346.3 45.7 all-reduce.15
  1431.6 9.8 reduce-scatter.14
  1443.9 11.4 reduce-scatter.16
  1524.0 72.5 all-reduce.13
  1611.1 76.1 reduce-scatter.8
  1691.3 167.7 reduce-scatter.6
  1863.2 213.6 reduce-scatter.10
  2080.8 213.6 reduce-scatter.12
  2297.6 28.9 all-reduce.7
Sparse Core Ops, SparseCore 1:
  427.4 103.1 all-gather.24
  532.6 100.1 all-gather.26
  644.1 42.9 all-gather.22
  805.2 81.8 all-gather.28
  1057.1 103.1 all-gather.24
  1162.4 100.1 all-gather.26
  1274.0 42.9 all-gather.22
  1434.9 81.6 all-gather.28
where the time goes:
time: 2380 us; the launch traced here: 2370 us
  waiting for transfers between devices  1700 us (71%)
  matrix products  374 us (16%)
  local copies, waits for them, and re-layouts  127 us (5%)
  other arithmetic  73.1 us (3%)
  blocking collectives  61 us (3%)
    reduce_scatter x1, waiting for transfers between devices, per_device(): lax.psum_scatter(weight_grads[2], 'shard', scatter_dimension=0, tiled=True)  218 us
    reduce_scatter x1, waiting for transfers between devices, per_device(): lax.psum_scatter(weight_grads[3], 'shard', scatter_dimension=1, tiled=True)  218 us
    all_gather x2, waiting for transfers between devices, one_micro(): lax.all_gather(fc1_weight, 'shard', axis=0, tiled=True)  181 us
    reduce_scatter x1, waiting for transfers between devices, per_device(): lax.psum_scatter(weight_grads[0], 'shard', scatter_dimension=1, tiled=True)  172 us
    psum x2, waiting for transfers between devices, one_micro(): lax.psum(jnp.dot(mixed, full_proj, preferred_element_type=jnp.float32), '...  148 us
    psum x2, waiting for transfers between devices, one_micro(): lax.psum(jnp.einsum('rf,df->rd', d_pre, back_first, preferred_element_typ...  112 us
    all_gather x2, waiting for transfers between devices, one_micro(): lax.all_gather(qkv_weight, 'shard', axis=1, tiled=True)  111 us
    all_gather x1, waiting for transfers between devices, per_device(): lax.all_gather(fc1_weight, 'shard', axis=0, tiled=True)  103 us
  transfers between devices with their start and end apart: 33, of which 24 were waited for; matrix products, arithmetic and copies ran while one was open for 17% of the time, Pallas kernels for 0%

commit v1 on v0

--- a/solution.py
+++ b/solution.py
@@ -8,6 +8,18 @@
 norm_epsilon = 1e-06
 gelu_factor = 1.702
 rope_base = 10000.0
+
+
+def doubled_up(x, axis, dim):
+    ways, here, step = (lax.axis_size(axis), lax.axis_index(axis), x.shape[dim])
+    line, have = (x, 1)
+    while have < ways:
+        line = jnp.concatenate(
+            [line, lax.ppermute(line, axis, [(d, (d - have) % ways) for d in range(ways)])],
+            axis=dim,
+        )
+        have = 2 * have
+    return jnp.roll(line, here * step, axis=dim)
 
 
 def norm_stats(values):
@@ -134,7 +146,7 @@
     head_count = inner_width // HDIM
     offset = lax.axis_index("ctx") * local_len
     full_qkv, full_proj, full_first, full_second = (
-        lax.all_gather(qkv_weight, "shard", axis=1, tiled=True),
+        doubled_up(qkv_weight, "shard", 1),
         lax.all_gather(proj_weight, "shard", axis=1, tiled=True),
         lax.all_gather(fc1_weight, "shard", axis=0, tiled=True),
         lax.all_gather(fc2_weight, "shard", axis=1, tiled=True),

time: 2380 us -> 2400 us (level)
    ppermute x0 -> x3, waiting for transfers between devices: none -> 240 us  [doubled_up(): lax.ppermute(line, axis, [(d, (d - have) % ways) for d in range(ways)])]
    all_gather x1, waiting for transfers between devices: 99.7 us -> 0.02 us  [per_device(): lax.all_gather(fc2_weight, 'shard', axis=1, tiled=True)]
    all_gather x1 -> x0, waiting for transfers between devices: 73.1 us -> none  [per_device(): lax.all_gather(qkv_weight, 'shard', axis=1, tiled=True)]
    all_gather x1, waiting for transfers between devices: 46.6 us -> 0.01 us  [per_device(): lax.all_gather(proj_weight, 'shard', axis=1, tiled=True)]
    all_gather x1, waiting for transfers between devices: 103 us -> 76.2 us  [per_device(): lax.all_gather(fc1_weight, 'shard', axis=0, tiled=True)]
  transfers between devices with their start and end apart: 33 -> 35, of which waited for: 24 -> 24; matrix products, arithmetic and copies ran while one was open for 17% -> 17% of each run, Pallas kernels for 0% -> 0%
where the time goes in v1:
time: 2400 us; the launch traced here: 2390 us
  waiting for transfers between devices  1700 us (71%)
  matrix products  374 us (16%)
  local copies, waits for them, and re-layouts  145 us (6%)
  other arithmetic  75.8 us (3%)
  blocking collectives  61 us (3%)
    ppermute x3, waiting for transfers between devices, doubled_up(): lax.ppermute(line, axis, [(d, (d - have) % ways) for d in range(ways)])  240 us
    reduce_scatter x1, waiting for transfers between devices, per_device(): lax.psum_scatter(weight_grads[2], 'shard', scatter_dimension=0, tiled=True)  218 us
    reduce_scatter x1, waiting for transfers between devices, per_device(): lax.psum_scatter(weight_grads[3], 'shard', scatter_dimension=1, tiled=True)  218 us
    all_gather x2, waiting for transfers between devices, one_micro(): lax.all_gather(fc1_weight, 'shard', axis=0, tiled=True)  181 us
    reduce_scatter x1, waiting for transfers between devices, per_device(): lax.psum_scatter(weight_grads[0], 'shard', scatter_dimension=1, tiled=True)  172 us
    psum x2, waiting for transfers between devices, one_micro(): lax.psum(jnp.dot(mixed, full_proj, preferred_element_type=jnp.float32), '...  148 us
    psum x2, waiting for transfers between devices, one_micro(): lax.psum(jnp.einsum('rf,df->rd', d_pre, back_first, preferred_element_typ...  122 us
    all_gather x2, waiting for transfers between devices, one_micro(): lax.all_gather(qkv_weight, 'shard', axis=1, tiled=True)  111 us
  transfers between devices with their start and end apart: 35, of which 24 were waited for; matrix products, arithmetic and copies ran while one was open for 17% of the time, Pallas kernels for 0%

profile of v1, /device:TPU:0, one launch (start us, length us, event | category | flops | bytes accessed | tf_op | source)
XLA Modules:
  0.0 2389.1 jit_solution(8228977261901746416)
XLA Ops:
  10.2 6.0 collective-permute-start
  16.3 20.0 collective-permute-done
  37.5 40.4 %collective-permute-done.1 = bf16[3,320,640]{2,1,0:T(8,128)(2,1)S(1)} collective-permute-done((bf16[3,320,640]{2,1,0:T(8,128)(2,1)S(1)}, bf16[3,320,640]{2,1,0:T(8,128)(2,1)S(1)}, u32[]{:S(2)}, u32[]{:S(2)}) %collective-permute-start.1) | collective-permute-done | bytes 1228832 | tf_op jit(solution)/shard_map/ppermute | solution.py:18
  82.7 3.5 copy.93
  86.2 179.1 %collective-permute-done.2 = bf16[3,640,640]{2,1,0:T(8,128)(2,1)} collective-permute-done((bf16[3,640,640]{2,1,0:T(8,128)(2,1)}, bf16[3,640,640]{2,1,0:T(8,128)(2,1)}, u32[]{:S(2)}, u32[]{:S(2)}) %collective-permute-start.2) | collective-permute-done | bytes 2457632 | tf_op jit(solution)/shard_map/ppermute | solution.py:18
  265.3 3.3 constant_dynamic-update-slice_fusion.4
  271.6 3.7 constant_dynamic-update-slice_fusion
  275.3 5.8 constant_dynamic-slice_fusion.7
  281.1 9.7 copy.94
  290.8 76.2 %all-gather.12.cloned.1.call-done = bf16[1280,2560]{1,0:T(8,128)(2,1)} async-done(((bf16[160,2560]{1,0:T(8,128)(2,1)}), bf16[1280,2560]{1,0:T(8,128)(2,1)}) %all-gather.12.cloned.1.call-update) | async-done | bytes 6553616 | tf_op jit(solution)/shard_map/all_gather | solution.py:151
  367.0 1259.1 %while.96 = (s32[]{:T(128)}, f32[3,1280,640]{1,2,0:T(8,128)}, f32[640,1280]{1,0:T(8,128)}, f32[1280,2560]{1,0:T(8,128)}, f32[2560,1280]{1,0:T(8,128)}, /*index=5...) while((s32[]{:T(128)}, f32[3,1280,640]{1,2,0:T(8,128)}, ...), condition=%wide.region_30.31_spmd.clone, body=%wide.region_0.30_spmd.clone.sunk | while | flops 30925250560 | bytes 610404544 | solution.py:306
  368.1 5.4 add_bitcast_fusion.2
  381.1 3.6 add_convert_fusion.10
  391.9 4.4 all-gather.16.cloned.1.call-done
  400.4 40.0 %while.97 = (s32[]{:T(128)}, bf16[8,512,80]{1,2,0:T(8,128)(2,1)S(1)}, f32[8,512]{1,0:T(8,128)}, s32[8,512]{1,0:T(8,128)S(1)}, s32[8,1024]{1,0:T(8,128)S(1)}, /*i...) while((s32[]{:T(128)}, ...), condition=%wide.region_6.6_spmd, body=%wide.region_3.5_spmd.sunk | while | flops 172531200 | bytes 7069817 | solution.py:187
  440.5 4.4 fusion.163
  446.6 74.0 %all-reduce.10.cloned.1.call-done = f32[512,1280]{1,0:T(8,128)} async-done(((f32[512,1280]{1,0:T(8,128)}), f32[512,1280]{1,0:T(8,128)}) %all-reduce.10.cloned.1.call-update) | async-done | bytes 2621456 | tf_op jit(solution)/shard_map/while/body/eval_jaxpr/psum | solution.py:192
  523.6 8.4 fusion.165
  531.9 18.7 all-gather.22.cloned.1.call-done
  550.7 11.5 convert_reduce_fusion.10
  562.2 90.6 %all-gather.24.cloned.1.call-done = bf16[1280,2560]{1,0:T(8,128)(2,1)} async-done(((bf16[160,2560]{1,0:T(8,128)(2,1)}), bf16[1280,2560]{1,0:T(8,128)(2,1)}) %all-gather.24.cloned.1.call-update) | async-done | bytes 6553616 | tf_op jit(solution)/shard_map/while/body/eval_jaxpr/all_gather | solution.py:214
  652.8 8.7 fusion.166
  662.3 10.6 convolution_convert_fusion.6
  673.1 61.1 %all-reduce.12.cloned.1.call-done = f32[512,1280]{1,0:T(8,128)} async-done(((f32[512,1280]{1,0:T(8,128)}), f32[512,1280]{1,0:T(8,128)}) %all-reduce.12.cloned.1.call-update) | async-done | bytes 2621456 | tf_op jit(solution)/shard_map/while/body/eval_jaxpr/psum | solution.py:229
  740.0 4.4 convolution_convert_fusion.5
  745.8 75.7 %while.98 = (s32[]{:T(128)}, f32[8,512,80]{1,2,0:T(8,128)}, f32[8,1024,80]{1,2,0:T(8,128)}, f32[8,1024,80]{1,2,0:T(8,128)}, s32[8,512]{1,0:T(8,128)S(1)}, /*inde...) while((s32[]{:T(128)}, f32[8,512,80]{1,2,0:T(8,128)}, ...), condition=%wide.region_15.15_spmd, body=%wide.region_13.14_spmd.sunk | while | flops 424795648 | bytes 17794184 | solution.py:242
  823.0 12.0 convolution_add_fusion.8
  840.0 5.4 reduce-scatter.17.cloned.1.call-done
  851.1 55.9 %all-gather.26.cloned.1.call-done = bf16[3,1280,640]{2,1,0:T(8,128)(2,1)} async-done(((bf16[3,160,640]{2,1,0:T(8,128)(2,1)}), bf16[3,1280,640]{2,1,0:T(8,128)(2,1)}) %all-gather.26.cloned.1.call-update) | async-done | bytes 4915216 | tf_op jit(solution)/shard_map/while/body/eval_jaxpr/all_gather | solution.py:212
  906.9 7.3 convolution_bitcast_fusion.3
  914.3 9.1 convolution_add_fusion.7
  927.4 6.4 bitcast_add_fusion.2
  933.8 53.1 %all-reduce.14.cloned.1.call-done = f32[512,1280]{1,0:T(8,128)} async-done(((f32[512,1280]{1,0:T(8,128)}), f32[512,1280]{1,0:T(8,128)}) %all-reduce.14.cloned.1.call-update) | async-done | bytes 2621456 | tf_op jit(solution)/shard_map/while/body/eval_jaxpr/psum | solution.py:266
  990.0 4.1 fusion.170
  995.4 5.4 add_bitcast_fusion.2
  1008.4 3.4 add_convert_fusion.10
  1019.0 6.6 all-gather.16.cloned.1.call-done
  1029.7 40.0 %while.97 = (s32[]{:T(128)}, bf16[8,512,80]{1,2,0:T(8,128)(2,1)S(1)}, f32[8,512]{1,0:T(8,128)}, s32[8,512]{1,0:T(8,128)S(1)}, s32[8,1024]{1,0:T(8,128)S(1)}, /*i...) while((s32[]{:T(128)}, ...), condition=%wide.region_6.6_spmd, body=%wide.region_3.5_spmd.sunk | while | flops 172531200 | bytes 7069817 | solution.py:187
  1069.8 4.4 fusion.163
  1075.9 74.0 %all-reduce.10.cloned.1.call-done = f32[512,1280]{1,0:T(8,128)} async-done(((f32[512,1280]{1,0:T(8,128)}), f32[512,1280]{1,0:T(8,128)}) %all-reduce.10.cloned.1.call-update) | async-done | bytes 2621456 | tf_op jit(solution)/shard_map/while/body/eval_jaxpr/psum | solution.py:192
  1152.9 8.4 fusion.165
  1161.2 19.1 all-gather.22.cloned.1.call-done
  1180.3 11.5 convert_reduce_fusion.10
  1191.8 90.8 %all-gather.24.cloned.1.call-done = bf16[1280,2560]{1,0:T(8,128)(2,1)} async-done(((bf16[160,2560]{1,0:T(8,128)(2,1)}), bf16[1280,2560]{1,0:T(8,128)(2,1)}) %all-gather.24.cloned.1.call-update) | async-done | bytes 6553616 | tf_op jit(solution)/shard_map/while/body/eval_jaxpr/all_gather | solution.py:214
  1282.6 8.7 fusion.166
  1292.1 10.6 convolution_convert_fusion.6
  1303.0 61.1 %all-reduce.12.cloned.1.call-done = f32[512,1280]{1,0:T(8,128)} async-done(((f32[512,1280]{1,0:T(8,128)}), f32[512,1280]{1,0:T(8,128)}) %all-reduce.12.cloned.1.call-update) | async-done | bytes 2621456 | tf_op jit(solution)/shard_map/while/body/eval_jaxpr/psum | solution.py:229
  1369.8 4.6 convolution_convert_fusion.5
  1375.7 75.8 %while.98 = (s32[]{:T(128)}, f32[8,512,80]{1,2,0:T(8,128)}, f32[8,1024,80]{1,2,0:T(8,128)}, f32[8,1024,80]{1,2,0:T(8,128)}, s32[8,512]{1,0:T(8,128)S(1)}, /*inde...) while((s32[]{:T(128)}, f32[8,512,80]{1,2,0:T(8,128)}, ...), condition=%wide.region_15.15_spmd, body=%wide.region_13.14_spmd.sunk | while | flops 424795648 | bytes 17794184 | solution.py:242
  1452.7 16.3 convolution_add_fusion.8
  1480.9 55.6 %all-gather.26.cloned.1.call-done = bf16[3,1280,640]{2,1,0:T(8,128)(2,1)} async-done(((bf16[3,160,640]{2,1,0:T(8,128)(2,1)}), bf16[3,1280,640]{2,1,0:T(8,128)(2,1)}) %all-gather.26.cloned.1.call-update) | async-done | bytes 4915216 | tf_op jit(solution)/shard_map/while/body/eval_jaxpr/all_gather | solution.py:212
  1536.4 7.2 convolution_bitcast_fusion.3
  1543.8 11.9 convolution_add_fusion.7
  1559.7 8.1 bitcast_add_fusion.2
  1567.8 48.6 %all-reduce.14.cloned.1.call-done = f32[512,1280]{1,0:T(8,128)} async-done(((f32[512,1280]{1,0:T(8,128)}), f32[512,1280]{1,0:T(8,128)}) %all-reduce.14.cloned.1.call-update) | async-done | bytes 2621456 | tf_op jit(solution)/shard_map/while/body/eval_jaxpr/psum | solution.py:266
  1619.5 4.1 fusion.170
  1626.2 4.6 copy.96
  1630.9 11.3 copy.95
  1643.0 14.0 copy.97
  1657.1 50.0 %reduce-scatter.9.cloned.1.call-done = f32[640,160]{0,1:T(8,128)} async-done(((f32[640,1280]{0,1:T(8,128)}), f32[640,160]{0,1:T(8,128)}) %reduce-scatter.9.cloned.1.call-update) | async-done | bytes 409616 | tf_op jit(solution)/shard_map/reduce_scatter | solution.py:316
  1707.1 172.0 %reduce-scatter.7.cloned.1.call-done = f32[3,160,640]{2,1,0:T(8,128)} async-done(((f32[3,1280,640]{2,1,0:T(8,128)}), f32[3,160,640]{2,1,0:T(8,128)}) %reduce-scatter.7.cloned.1.call-update) | async-done | bytes 1228816 | tf_op jit(solution)/shard_map/reduce_scatter | solution.py:315
  1879.1 217.8 %reduce-scatter.11.cloned.1.call-done = f32[160,2560]{1,0:T(8,128)} async-done(((f32[1280,2560]{1,0:T(8,128)}), f32[160,2560]{1,0:T(8,128)}) %reduce-scatter.11.cloned.1.call-update) | async-done | bytes 1638416 | tf_op jit(solution)/shard_map/reduce_scatter | solution.py:317
  2096.9 217.8 %reduce-scatter.13.cloned.1.call-done = f32[2560,160]{0,1:T(8,128)} async-done(((f32[2560,1280]{0,1:T(8,128)}), f32[2560,160]{0,1:T(8,128)}) %reduce-scatter.13.cloned.1.call-update) | async-done | bytes 1638416 | tf_op jit(solution)/shard_map/reduce_scatter | solution.py:318
  2314.8 61.0 %all-reduce = (f32[1280]{0:T(1024)}, f32[1280]{0:T(1024)}, f32[3,640]{1,0:T(4,128)}, f32[1280]{0:T(1024)}, f32[1280]{0:T(1024)}, /*index=5*/f32[1280]{0:T(1024)}, f32[2560]{0:T(1024)}, f32[1280]{0:T(1024)}) all-reduce(f32[1280]{0:T(1024)S(1)} %copy-done.56, ...), channel_id=1, replica_groups=mesh['shard'=8,'ctx'=2,'tp'=2] {'shard','ctx'}, use_global_device_ids=true, to_apply=%region_31.32 | all-reduce | flops 12160 | bytes 97280 | tf_op jit(solution)/shard_map/psum | solution.py:309
  (709 shorter events, 351.2 us)
Async XLA Ops:
  8.0 69.9 %copy-start.16 = (bf16[3,160,640]{2,1,0:T(8,128)(2,1)S(1)}, bf16[3,160,640]{2,1,0:T(8,128)(2,1)}, u32[]{:S(2)}) copy-start(bf16[3,160,640]{2,1,0:T(8,128)(2,1)} %param.25) | copy-start | bytes 1843204
  8.0 74.7 %all-gather.10.cloned.1.call-start = ((), (), s32[]{:S(2)}) async-start(), calls=%async_computation.6 | async-start | bytes 1843200 | tf_op jit(solution)/shard_map/all_gather | solution.py:150
  8.8 272.4 %all-gather.14.cloned.1.call-start = ((), (), s32[]{:S(2)}) async-start(), calls=%async_computation.8 | async-start | bytes 7372800 | tf_op jit(solution)/shard_map/all_gather | solution.py:152
  9.5 357.5 %all-gather.12.cloned.1.call-start = ((), (), s32[]{:S(2)}) async-start(), calls=%async_computation.7 | async-start | bytes 7372800 | tf_op jit(solution)/shard_map/all_gather | solution.py:151
  10.2 26.0 %collective-permute-start = (bf16[3,160,640]{2,1,0:T(8,128)(2,1)}, bf16[3,160,640]{2,1,0:T(8,128)(2,1)S(1)}, u32[]{:S(2)}, u32[]{:S(2)}) collective-permute-start(bf16[3,160,640]{2,1,0:T(8,128)(2,1)} %param.25), channel_id=1, source_target_pairs={{0,28},{4,0},{8,4},{12,8},{16,12},{20,16},{24,20},{28,24},{1,29},{... | collective-permute-start | bytes 1843208 | tf_op jit(solution)/shard_map/ppermute | solution.py:18
  37.5 42.2 %copy-start.63 = (s32[3,2,1,1024]{3,2,1,0:T(1,128)S(1)}, s32[3,2,1,1024]{3,2,1,0:T(1,128)}, u32[]{:S(2)}) copy-start(s32[3,2,1,1024]{3,2,1,0:T(1,128)} %param.22) | copy-start | bytes 73732
  37.5 40.5 %collective-permute-start.1 = (bf16[3,320,640]{2,1,0:T(8,128)(2,1)S(1)}, bf16[3,320,640]{2,1,0:T(8,128)(2,1)S(1)}, u32[]{:S(2)}, u32[]{:S(2)}) collective-permute-start(bf16[3,320,640]{2,1,0:T(8,128)(2,1)S(1)} %pad_maximum_fusion.7), channel_id=1, source_target_pairs={{0,24},{4,28},{8,0},{12,4},{16,8},{20,12},{24,16},{28,20},{1,25},{... | collective-permute-start | bytes 3686408 | tf_op jit(solution)/shard_map/ppermute | solution.py:18
  79.6 185.8 %collective-permute-start.2 = (bf16[3,640,640]{2,1,0:T(8,128)(2,1)}, bf16[3,640,640]{2,1,0:T(8,128)(2,1)}, u32[]{:S(2)}, u32[]{:S(2)}) collective-permute-start(bf16[3,640,640]{2,1,0:T(8,128)(2,1)} %pad_maximum_fusion.6), channel_id=1, source_target_pairs={{0,16},{4,20},{8,24},{12,28},{16,0},{20,4},{24,8},{28,12},{1,17},{... | collective-permute-start | bytes 7372808 | tf_op jit(solution)/shard_map/ppermute | solution.py:18
  281.0 85.9 %copy-start = (bf16[2,1,512,1280]{3,2,1,0:T(8,128)(2,1)S(1)}, bf16[2,1,512,1280]{3,2,1,0:T(8,128)(2,1)}, u32[]{:S(2)}) copy-start(bf16[2,1,512,1280]{3,2,1,0:T(8,128)(2,1)} %param.21) | copy-start | bytes 7864324
  281.1 85.9 %copy-start.21 = (f32[1280]{0:T(1024)S(1)}, f32[1280]{0:T(1024)}, u32[]{:S(2)}) copy-start(f32[1280]{0:T(1024)} %param.29) | copy-start | bytes 15364
  281.1 85.9 %copy-start.22 = (f32[1280]{0:T(1024)S(1)}, f32[1280]{0:T(1024)}, u32[]{:S(2)}) copy-start(f32[1280]{0:T(1024)} %param.23) | copy-start | bytes 15364
  281.1 85.9 %copy-start.28 = (f32[1280]{0:T(1024)S(1)}, f32[1280]{0:T(1024)}, u32[]{:S(2)}) copy-start(f32[1280]{0:T(1024)} %param.30) | copy-start | bytes 15364
  281.1 85.9 %copy-start.59 = (f32[1280]{0:T(1024)S(1)}, f32[1280]{0:T(1024)}, u32[]{:S(2)}) copy-start(f32[1280]{0:T(1024)} %param.24) | copy-start | bytes 15364
  281.1 85.9 %copy-start.61 = (f32[1280]{0:T(1024)S(1)}, f32[1280]{0:T(1024)}, u32[]{:S(2)}) copy-start(f32[1280]{0:T(1024)} %param.28) | copy-start | bytes 15364
  281.1 85.9 %copy-start.64 = (f32[2560]{0:T(1024)S(1)}, f32[2560]{0:T(1024)}, u32[]{:S(2)}) copy-start(f32[2560]{0:T(1024)} %param.32) | copy-start | bytes 30724
  281.1 85.9 %copy-start.66 = (f32[3,640]{1,0:T(4,128)S(1)}, f32[3,640]{1,0:T(4,128)}, u32[]{:S(2)}) copy-start(f32[3,640]{1,0:T(4,128)} %param.26) | copy-start | bytes 23044
  367.3 20.5 copy-start.57
  367.3 20.5 all-gather.18.cloned.1.call-start
  376.5 19.8 all-gather.16.cloned.1.call-start
  384.7 135.9 %all-reduce.10.cloned.1.call-start = ((), (), s32[]{:S(2)}) async-start(), calls=%async_computation.17 | async-start | bytes 5242880 | tf_op jit(solution)/shard_map/while/body/eval_jaxpr/psum | solution.py:192
  444.9 105.8 %all-gather.22.cloned.1.call-start = ((), (), s32[]{:S(2)}) async-start(), calls=%async_computation.18 | async-start | bytes 7372800 | tf_op jit(solution)/shard_map/while/body/eval_jaxpr/all_gather | solution.py:215
  445.5 207.4 %all-gather.24.cloned.1.call-start = ((), (), s32[]{:S(2)}) async-start(), calls=%async_computation.19 | async-start | bytes 7372800 | tf_op jit(solution)/shard_map/while/body/eval_jaxpr/all_gather | solution.py:214
  446.0 288.2 %all-reduce.12.cloned.1.call-start = ((), (), s32[]{:S(2)}) async-start(), calls=%async_computation.20 | async-start | bytes 5242880 | tf_op jit(solution)/shard_map/while/body/eval_jaxpr/psum | solution.py:229
  661.6 78.4 %all-gather.20.cloned.1.call-start = ((), (), s32[]{:S(2)}) async-start(), calls=%async_computation.16 | async-start | bytes 1843200 | tf_op jit(solution)/shard_map/while/body/eval_jaxpr/all_gather | solution.py:213
  662.2 172.8 %all-reduce.16.cloned.1.call-start = ((), (), s32[]{:S(2)}) async-start(), calls=%async_computation.25 | async-start | bytes 2621440 | tf_op jit(solution)/shard_map/while/body/eval_jaxpr/psum | solution.py:202
  672.9 164.8 %reduce-scatter.15.cloned.1.call-start = ((), (), s32[]{:S(2)}) async-start(), calls=%async_computation.21 | async-start | bytes 3932160 | tf_op jit(solution)/shard_map/while/body/eval_jaxpr/reduce_scatter | solution.py:250
  821.6 23.9 reduce-scatter.17.cloned.1.call-start
  822.1 84.8 %all-gather.26.cloned.1.call-start = ((), (), s32[]{:S(2)}) async-start(), calls=%async_computation.23 | async-start | bytes 5529600 | tf_op jit(solution)/shard_map/while/body/eval_jaxpr/all_gather | solution.py:212
  822.9 164.0 %all-reduce.14.cloned.1.call-start = ((), (), s32[]{:S(2)}) async-start(), calls=%async_computation.24 | async-start | bytes 5242880 | tf_op jit(solution)/shard_map/while/body/eval_jaxpr/psum | solution.py:266
  933.8 56.1 %copy-start.51 = (f32[1280]{0:T(1024)S(1)}, f32[1280]{0:T(1024)}, u32[]{:S(2)}) copy-start(f32[1280]{0:T(1024)} %get-tuple-element.1512) | copy-start | bytes 15364 | tf_op jit(solution)/shard_map/while
  933.8 56.1 %copy-start.54 = (f32[1280]{0:T(1024)S(1)}, f32[1280]{0:T(1024)}, u32[]{:S(2)}) copy-start(f32[1280]{0:T(1024)} %get-tuple-element.1511) | copy-start | bytes 15364 | tf_op jit(solution)/shard_map/while
  933.8 56.1 %copy-start.23 = (f32[1280]{0:T(1024)S(1)}, f32[1280]{0:T(1024)}, u32[]{:S(2)}) copy-start(f32[1280]{0:T(1024)} %get-tuple-element.1772) | copy-start | bytes 15364 | tf_op jit(solution)/shard_map/while
  994.6 20.3 copy-start.57
  994.6 20.3 all-gather.18.cloned.1.call-start
  1003.8 21.8 all-gather.16.cloned.1.call-start
  1011.8 138.1 %all-reduce.10.cloned.1.call-start = ((), (), s32[]{:S(2)}) async-start(), calls=%async_computation.17 | async-start | bytes 5242880 | tf_op jit(solution)/shard_map/while/body/eval_jaxpr/psum | solution.py:192
  1074.2 106.1 %all-gather.22.cloned.1.call-start = ((), (), s32[]{:S(2)}) async-start(), calls=%async_computation.18 | async-start | bytes 7372800 | tf_op jit(solution)/shard_map/while/body/eval_jaxpr/all_gather | solution.py:215
  1074.9 207.7 %all-gather.24.cloned.1.call-start = ((), (), s32[]{:S(2)}) async-start(), calls=%async_computation.19 | async-start | bytes 7372800 | tf_op jit(solution)/shard_map/while/body/eval_jaxpr/all_gather | solution.py:214
  1075.7 288.4 %all-reduce.12.cloned.1.call-start = ((), (), s32[]{:S(2)}) async-start(), calls=%async_computation.20 | async-start | bytes 5242880 | tf_op jit(solution)/shard_map/while/body/eval_jaxpr/psum | solution.py:229
  1291.4 78.4 %all-gather.20.cloned.1.call-start = ((), (), s32[]{:S(2)}) async-start(), calls=%async_computation.16 | async-start | bytes 1843200 | tf_op jit(solution)/shard_map/while/body/eval_jaxpr/all_gather | solution.py:213
  1292.0 177.0 %all-reduce.16.cloned.1.call-start = ((), (), s32[]{:S(2)}) async-start(), calls=%async_computation.25 | async-start | bytes 2621440 | tf_op jit(solution)/shard_map/while/body/eval_jaxpr/psum | solution.py:202
  1302.7 169.0 %reduce-scatter.15.cloned.1.call-start = ((), (), s32[]{:S(2)}) async-start(), calls=%async_computation.21 | async-start | bytes 3932160 | tf_op jit(solution)/shard_map/while/body/eval_jaxpr/reduce_scatter | solution.py:250
  1451.5 23.7 reduce-scatter.17.cloned.1.call-start
  1452.1 84.4 %all-gather.26.cloned.1.call-start = ((), (), s32[]{:S(2)}) async-start(), calls=%async_computation.23 | async-start | bytes 5529600 | tf_op jit(solution)/shard_map/while/body/eval_jaxpr/all_gather | solution.py:212
  1452.7 163.7 %all-reduce.14.cloned.1.call-start = ((), (), s32[]{:S(2)}) async-start(), calls=%async_computation.24 | async-start | bytes 5242880 | tf_op jit(solution)/shard_map/while/body/eval_jaxpr/psum | solution.py:266
  1452.7 16.3 copy-start.62
  1543.8 12.1 copy-start.2
  1543.8 12.1 copy-start.11
  1567.8 51.6 %copy-start.51 = (f32[1280]{0:T(1024)S(1)}, f32[1280]{0:T(1024)}, u32[]{:S(2)}) copy-start(f32[1280]{0:T(1024)} %get-tuple-element.1512) | copy-start | bytes 15364 | tf_op jit(solution)/shard_map/while
  1567.8 51.6 %copy-start.54 = (f32[1280]{0:T(1024)S(1)}, f32[1280]{0:T(1024)}, u32[]{:S(2)}) copy-start(f32[1280]{0:T(1024)} %get-tuple-element.1511) | copy-start | bytes 15364 | tf_op jit(solution)/shard_map/while
  1567.8 51.6 %copy-start.23 = (f32[1280]{0:T(1024)S(1)}, f32[1280]{0:T(1024)}, u32[]{:S(2)}) copy-start(f32[1280]{0:T(1024)} %get-tuple-element.1772) | copy-start | bytes 15364 | tf_op jit(solution)/shard_map/while
  1626.1 81.0 %reduce-scatter.9.cloned.1.call-start = ((), (), s32[]{:S(2)}) async-start(), calls=%async_computation.10 | async-start | bytes 3686400 | tf_op jit(solution)/shard_map/reduce_scatter | solution.py:316
  1630.8 248.3 %reduce-scatter.7.cloned.1.call-start = ((), (), s32[]{:S(2)}) async-start(), calls=%async_computation.9 | async-start | bytes 11059200 | tf_op jit(solution)/shard_map/reduce_scatter | solution.py:315
  1642.2 454.8 %reduce-scatter.11.cloned.1.call-start = ((), (), s32[]{:S(2)}) async-start(), calls=%async_computation.11 | async-start | bytes 14745600 | tf_op jit(solution)/shard_map/reduce_scatter | solution.py:317
  1642.9 671.8 %reduce-scatter.13.cloned.1.call-start = ((), (), s32[]{:S(2)}) async-start(), calls=%async_computation.12 | async-start | bytes 14745600 | tf_op jit(solution)/shard_map/reduce_scatter | solution.py:318
  1657.0 657.7 %copy-start.33 = (f32[2560]{0:T(1024)S(1)}, f32[2560]{0:T(1024)}, u32[]{:S(2)}) copy-start(f32[2560]{0:T(1024)} %get-tuple-element.1896) | copy-start | bytes 30724
  1657.0 657.7 %copy-start.37 = (f32[3,640]{1,0:T(4,128)S(1)}, f32[3,640]{1,0:T(4,128)}, u32[]{:S(2)}) copy-start(f32[3,640]{1,0:T(4,128)} %get-tuple-element.1892) | copy-start | bytes 23044
  1657.0 657.7 %copy-start.41 = (f32[1280]{0:T(1024)S(1)}, f32[1280]{0:T(1024)}, u32[]{:S(2)}) copy-start(f32[1280]{0:T(1024)} %get-tuple-element.1897) | copy-start | bytes 15364
  1657.0 657.7 %copy-start.44 = (f32[1280]{0:T(1024)S(1)}, f32[1280]{0:T(1024)}, u32[]{:S(2)}) copy-start(f32[1280]{0:T(1024)} %get-tuple-element.1895) | copy-start | bytes 15364
  1657.0 657.7 %copy-start.47 = (f32[1280]{0:T(1024)S(1)}, f32[1280]{0:T(1024)}, u32[]{:S(2)}) copy-start(f32[1280]{0:T(1024)} %get-tuple-element.1894) | copy-start | bytes 15364
  1657.0 657.7 %copy-start.50 = (f32[1280]{0:T(1024)S(1)}, f32[1280]{0:T(1024)}, u32[]{:S(2)}) copy-start(f32[1280]{0:T(1024)} %get-tuple-element.1893) | copy-start | bytes 15364
  1657.0 657.7 %copy-start.53 = (f32[1280]{0:T(1024)S(1)}, f32[1280]{0:T(1024)}, u32[]{:S(2)}) copy-start(f32[1280]{0:T(1024)} %get-tuple-element.1891) | copy-start | bytes 15364
  1657.1 657.7 %copy-start.56 = (f32[1280]{0:T(1024)S(1)}, f32[1280]{0:T(1024)}, u32[]{:S(2)}) copy-start(f32[1280]{0:T(1024)} %get-tuple-element.1890) | copy-start | bytes 15364
  1657.1 718.7 %all-reduce.8.cloned.1.call-start = ((), (), s32[]{:S(2)}) async-start(), calls=%async_computation.13 | async-start | bytes 9830400 | tf_op jit(solution)/shard_map/psum | solution.py:320
  (88 other events, 426.6 us)
Sparse Core Ops, SparseCore 0:
  11.0 57.5 all-gather.9
  70.9 192.6 all-gather.13
  265.7 101.2 all-gather.11
  376.6 7.5 all-gather.17
  385.7 10.5 all-gather.15
  445.0 75.5 all-reduce.9
  661.7 72.5 all-reduce.11
  736.7 45.7 all-reduce.15
  821.7 10.0 reduce-scatter.14
  833.9 11.4 reduce-scatter.16
  914.3 72.5 all-reduce.13
  1004.0 9.3 all-gather.17
  1015.0 10.5 all-gather.15
  1074.3 75.5 all-reduce.9
  1291.5 72.5 all-reduce.11
  1366.3 45.7 all-reduce.15
  1451.6 9.9 reduce-scatter.14
  1463.8 11.3 reduce-scatter.16
  1543.8 72.5 all-reduce.13
  1630.9 76.1 reduce-scatter.8
  1711.2 167.9 reduce-scatter.6
  1883.2 213.6 reduce-scatter.10
  2101.0 213.6 reduce-scatter.12
  2317.6 28.9 all-reduce.7
Sparse Core Ops, SparseCore 1:
  447.5 103.1 all-gather.21
  552.7 100.1 all-gather.23
  664.3 42.9 all-gather.19
  825.1 81.8 all-gather.25
  1077.2 103.1 all-gather.21
  1182.5 100.1 all-gather.23
  1294.1 42.9 all-gather.19
  1454.7 81.6 all-gather.25
